TPU v7x, 32 devices: a whole 2x2x4 slice. The times are simulated.
32 devices in a mesh: order: 2 (over core), tok: 16 (over z, y, x).
Axes of the slice: x: 2, y: 2, z: 4, core: 2. Of those that a mesh axis runs over, the one named last changes fastest.
Arguments:
- queries: bfloat16 [65536, 512], P(('order', 'tok')), may hold values from -6 to 6
- key_tokens: bfloat16 [65536, 512], P(('order', 'tok')), may hold values from -6 to 6
- value_tokens: bfloat16 [65536, 512], P(('order', 'tok')), may hold values from -6 to 6
- learn_rates: float32 [65536], P(('order', 'tok')), may hold values from 0.02 to 0.2
- fast_init: float32 [512, 1536], replicated, may hold values from -0.25 to 0.25
- out_gain: float32 [512], replicated, may hold values from 0.5 to 1.5
Outputs:
- output: bfloat16 [65536, 512], P(('order', 'tok'))
All inputs are finite; a program needn't handle non-finite values.
Results may differ from a plain program's by a relative error of at most 0.015.
Values may be sent and summed in bfloat16 or wider, within the bound.
A program may use at most 128 MiB of HBM per device.

v0:
```python
import jax
import jax.numpy as jnp
from jax import lax
from jax.sharding import PartitionSpec as P


def prefix(x, axis, join, neutral):
    place = lax.axis_index(axis)
    gathered = lax.all_gather(x.astype(jnp.bfloat16), axis)
    state = jnp.zeros_like(x) + jnp.asarray(neutral, x.dtype)

    def one(lap, state):
        return join(state, lax.dynamic_index_in_dim(gathered, lap, 0, False).astype(x.dtype))

    return lax.fori_loop(0, place, one, state)


def gate_up(rows_in, weights_bf):
    width = weights_bf.shape[0]
    both_parts = jnp.dot(rows_in, weights_bf[:, : 2 * width], preferred_element_type=jnp.float32)
    return (both_parts[:, :width], both_parts[:, width:])


def backward_terms(key_rows, target, weights_bf):
    width = weights_bf.shape[0]
    gate_pre, up_pre = gate_up(key_rows, weights_bf)
    squash = jax.nn.sigmoid(gate_pre)
    activated = gate_pre * squash
    hidden = (activated * up_pre).astype(jnp.bfloat16)
    hidden_grad = lax.dot_general(
        target,
        weights_bf[:, 2 * width :],
        (((1,), (1,)), ((), ())),
        preferred_element_type=jnp.float32,
    )
    gate_grad = (hidden_grad * up_pre * squash * (1.0 + gate_pre * (1.0 - squash))).astype(
        jnp.bfloat16
    )
    up_grad = (hidden_grad * activated).astype(jnp.bfloat16)
    return (hidden, jnp.concatenate([gate_grad, up_grad], axis=1))


def local_term(key_rows, hidden, inner_grads, target):
    upper = lax.dot_general(
        key_rows, inner_grads, (((0,), (0,)), ((), ())), preferred_element_type=jnp.float32
    )
    lower = lax.dot_general(
        hidden, target, (((0,), (0,)), ((), ())), preferred_element_type=jnp.float32
    )
    return jnp.concatenate([upper, lower], axis=1)


def summed_whole(key_rows, target, weights_bf):
    hidden, inner_grads = backward_terms(key_rows, target, weights_bf)
    return lax.psum(local_term(key_rows, hidden, inner_grads, target), "tok")


def accumulate(earlier, later):
    return earlier + later


def apply_weights(query_rows, weights_bf, out_gain):
    width = weights_bf.shape[0]
    gate_pre, up_pre = gate_up(query_rows, weights_bf)
    hidden = (jax.nn.silu(gate_pre) * up_pre).astype(jnp.bfloat16)
    result = jnp.dot(hidden, weights_bf[:, 2 * width :], preferred_element_type=jnp.float32)
    norm_inv = lax.rsqrt(jnp.mean(result * result, axis=1, keepdims=True) + 1e-06)
    return (result * norm_inv * out_gain[None, :]).astype(jnp.bfloat16)


def shards(queries, key_tokens, value_tokens, learn_rates, fast_init, out_gain):
    group_rows = key_tokens.shape[0] * lax.axis_size("tok")
    factor = group_rows ** (-0.5)
    target = (-(learn_rates[:, None] * factor) * value_tokens.astype(jnp.float32)).astype(
        jnp.bfloat16
    )
    first_step = fast_init - summed_whole(key_tokens, target, fast_init.astype(jnp.bfloat16))
    second_step = first_step - summed_whole(key_tokens, target, first_step.astype(jnp.bfloat16))
    change = second_step - fast_init
    earlier = prefix(change, "order", accumulate, jnp.zeros_like(change))
    closing_bf = (fast_init + earlier + change).astype(jnp.bfloat16)
    return apply_weights(queries, closing_bf, out_gain)


def solution(mesh):
    return jax.shard_map(
        shards,
        mesh=mesh,
        in_specs=(
            P(("order", "tok"), None),
            P(("order", "tok"), None),
            P(("order", "tok"), None),
            P(("order", "tok")),
            P(),
            P(),
        ),
        out_specs=P(("order", "tok"), None),
        check_vma=False,
    )
```

profile of v0, /device:TPU:0, one launch (start us, length us, event | category | flops | bytes accessed | tf_op | source)
XLA Modules:
  0.0 381.2 jit_solution(1011616236271366115)
XLA Ops:
  6.5 0.0 copy-start
  6.5 0.0 all-reduce.3.cloned.1.call-start
  6.5 0.8 multiply_negate_fusion
  7.4 2.1 convert_element_type.50
  9.5 0.0 copy-done
  9.5 0.0 copy-start.4
  9.5 2.4 fusion.24
  11.9 0.0 copy-done.4
  11.9 2.9 multiply_convert_fusion.6
  14.8 2.1 fusion.11
  16.9 2.3 fusion.18
  19.2 2.0 pad_maximum_fusion
  21.2 0.0 all-reduce.3.cloned.1.call-update
  21.2 0.2 all-reduce.5.cloned.1.call-start
  21.5 3.5 copy.10
  25.0 146.0 %all-reduce.3.cloned.1.call-done = f32[512,1536]{0,1:T(8,128)} async-done(((f32[512,1536]{0,1:T(8,128)}), f32[512,1536]{0,1:T(8,128)}) %all-reduce.3.cloned.1.call-update) | async-done | bytes 3145744 | tf_op jit(solution)/shard_map/psum | solution.py:55
  171.0 5.3 %fusion.38 = (bf16[512,1536]{0,1:T(8,128)(2,1)S(1)}, f32[512,1536]{0,1:T(8,128)}) fusion(f32[512,1536]{0,1:T(8,128)} %copy.10, f32[512,1536]{0,1:T(8,128)} %all-reduce.3.cloned.1.call-done), kind=kLoop, calls=%fused_computation.52 | loop fusion | flops 1572864 | bytes 11010048 | tf_op jit(solution)/shard_map/convert_element_type | solution.py:78
  176.3 0.0 copy-start.5
  176.3 2.4 convolution_bitcast_fusion.1
  178.7 0.0 copy-done.5
  178.7 3.2 multiply_convert_fusion.3
  181.9 2.1 fusion.12
  184.0 2.3 fusion.15
  186.4 2.0 pad_maximum_fusion.1
  188.3 0.0 copy-start.2
  188.3 0.0 all-reduce.5.cloned.1.call-update
  188.3 0.0 all-gather.3.cloned.1.call-start
  188.4 146.1 %all-reduce.5.cloned.1.call-done = f32[512,1536]{0,1:T(8,128)} async-done(((f32[512,1536]{0,1:T(8,128)}), f32[512,1536]{0,1:T(8,128)}) %all-reduce.5.cloned.1.call-update) | async-done | bytes 3145744 | tf_op jit(solution)/shard_map/psum | solution.py:55
  334.5 0.0 copy-done.2
  334.5 4.9 %fusion.21 = bf16[512,1536]{0,1:T(8,128)(2,1)} fusion(f32[512,1536]{0,1:T(8,128)S(1)} %copy-done.2, f32[512,1536]{0,1:T(8,128)} %get-tuple-element.42, f32[512,1536]{0,1:T(8,128)} %all-reduce.5.cloned.1.call-done), kind=kLoop, calls=%fused_computation.35 | loop fusion | flops 2359296 | bytes 11010048 | tf_op jit(solution)/shard_map/convert_element_type | solution.py:9
  339.4 0.0 all-gather.3.cloned.1.call-update
  339.4 11.4 %all-gather.3.cloned.1.call-done = bf16[1024,1536]{0,1:T(8,128)(2,1)} async-done(((bf16[512,1536]{0,1:T(8,128)(2,1)}), bf16[1024,1536]{0,1:T(8,128)(2,1)}) %all-gather.3.cloned.1.call-update) | async-done | bytes 3145744 | tf_op jit(solution)/shard_map/all_gather | solution.py:9
  350.9 4.6 %copy.13 = bf16[1024,1536]{1,0:T(8,128)(2,1)} copy(bf16[1024,1536]{0,1:T(8,128)(2,1)} %all-gather.3.cloned.1.call-done) | data formatting | bytes 6291456 | tf_op jit(solution)/shard_map/while | solution.py:15
  355.5 0.4 broadcast_in_dim.2
  355.9 0.2 while.10
  356.1 2.4 copy.11
  358.5 0.0 copy-start.6
  358.5 6.4 %add_convert_fusion = bf16[512,1536]{0,1:T(8,128)(2,1)S(1)} fusion(f32[512,1536]{0,1:T(8,128)} %copy.10, f32[512,1536]{0,1:T(8,128)} %copy.11, f32[512,1536]{0,1:T(8,128)} %get-tuple-element.42, f32[512,1536]{0,1:T(8,128)} %all-reduce.5.cloned.1.call-done), kind=kLoop, calls=%fused_computation.28 | loop fusion | flops 3932160 | bytes 14155776 | tf_op jit(solution)/shard_map/convert_element_type | solution.py:81
  364.8 0.0 copy-done.6
  364.9 2.4 convolution_bitcast_fusion
  367.2 0.0 copy-start.3
  367.2 1.7 multiply_reduce_fusion
  369.0 0.0 copy-done.3
  369.0 0.0 copy-start.1
  369.0 1.7 multiply_convert_fusion
  370.7 3.9 %copy.12 = bf16[2048,512]{1,0:T(8,128)(2,1)} copy(bf16[2048,512]{0,1:T(8,128)(2,1)} %multiply_convert_fusion) | data formatting | bytes 4194304 | tf_op jit(solution)/shard_map/convert_element_type | solution.py:68
  374.6 0.0 copy-done.1
  (1 shorter events, 0.0 us)
Async XLA Ops:
  6.5 2.9 copy-start
  6.5 164.5 %all-reduce.3.cloned.1.call-start = ((), (), s32[]{:S(2)}) async-start(), calls=%async_computation | async-start | bytes 6291456 | tf_op jit(solution)/shard_map/psum | solution.py:55
  9.5 2.5 copy-start.4
  21.2 313.3 %all-reduce.5.cloned.1.call-start = ((), (), s32[]{:S(2)}) async-start(), calls=%async_computation.1 | async-start | bytes 6291456 | tf_op jit(solution)/shard_map/psum | solution.py:55
  176.3 2.4 copy-start.5
  188.3 146.2 %copy-start.2 = (f32[512,1536]{0,1:T(8,128)S(1)}, f32[512,1536]{0,1:T(8,128)}, u32[]{:S(2)}) copy-start(f32[512,1536]{0,1:T(8,128)} %copy.10) | copy-start | bytes 9437188
  188.3 162.5 %all-gather.3.cloned.1.call-start = ((), (), s32[]{:S(2)}) async-start(), calls=%async_computation.2 | async-start | bytes 4718592 | tf_op jit(solution)/shard_map/all_gather | solution.py:9
  358.5 6.4 %copy-start.6 = (bf16[2048,512]{1,0:T(8,128)(2,1)S(1)}, bf16[2048,512]{1,0:T(8,128)(2,1)}, u32[]{:S(2)}) copy-start(bf16[2048,512]{1,0:T(8,128)(2,1)} %param.8) | copy-start | bytes 6291460
  367.2 1.7 copy-start.3
  369.0 5.7 %copy-start.1 = (bf16[2048,512]{1,0:T(8,128)(2,1)S(1)}, bf16[2048,512]{1,0:T(8,128)(2,1)}, u32[]{:S(2)}) copy-start(bf16[2048,512]{1,0:T(8,128)(2,1)} %param.9) | copy-start | bytes 6291460
Sparse Core Ops, SparseCore 0:
  21.4 149.5 all-reduce.2
  188.5 145.9 all-reduce.4
  339.6 11.2 all-gather.2
where the time goes:
time: 383 us; the launch traced here: 381 us
  waiting for transfers between devices  304 us (79%)
  other arithmetic  25.1 us (7%)
  matrix products  23.8 us (6%)
  local copies, waits for them, and re-layouts  14.8 us (4%)
  between operations  13.3 us (3%)
    psum x2, waiting for transfers between devices, summed_whole(): return lax.psum(local_term(key_rows, hidden, inner_grads, target), 'tok')  292 us
    all_gather x1, waiting for transfers between devices, prefix(): gathered = lax.all_gather(x.astype(jnp.bfloat16), axis)  11.4 us
  transfers between devices with their start and end apart: 3, of which 3 were waited for; matrix products, arithmetic and copies ran while one was open for 1% of the time, Pallas kernels for 0%

commit v1 on v0

--- a/solution.py
+++ b/solution.py
@@ -1,7 +1,15 @@
+import functools
+
 import jax
 import jax.numpy as jnp
 from jax import lax
+from jax.experimental import pallas as pl
+from jax.experimental.pallas import tpu as pltpu
 from jax.sharding import PartitionSpec as P
+
+CHUNKS = 2
+PARTS = 4
+MESH = pl.DeviceIdType.MESH
 
 
 def prefix(x, axis, join, neutral):
@@ -82,9 +90,333 @@
     return apply_weights(queries, closing_bf, out_gain)
 
 
+def tiles(mesh):
+    return mesh.shape["order"] == 2 and mesh.shape["tok"] == 16
+
+
+def plan():
+    compute = {"T": 1.0, "E": 0.9, "G": 0.8, "Q": 0.9}
+    wire = {"x": 0.0, "y": 0.0, "z": 0.0}
+    order, now = [], 0.0
+    ready, done = {}, set()
+    todo = []
+    for step in range(2):
+        for c in range(CHUNKS):
+            for part in range(PARTS):
+                todo.append(("E", step, c, part))
+            for m in (2, 0, 1):
+                todo.append(("G", step, c, m))
+    for c in range(CHUNKS):
+        for part in range(PARTS):
+            todo.append(("Q", 2, c, part))
+
+    def sent(links, us, latency):
+        arrive = 0.0
+        for link in links:
+            wire[link] = max(wire[link], now) + us
+            arrive = max(arrive, wire[link])
+        return arrive + latency
+
+    def blocked(op):
+        if op[0] == "G" or op[1] == 0:
+            return False
+        return not all((op[1] - 1, op[2], m) in done for m in range(3))
+
+    last = {0: 6, 1: 7}
+    while todo or ready:
+        due = sorted((when, key) for key, when in ready.items() if when <= now + 0.05)
+        if due:
+            key = due[0][1]
+            piece, stage = key[:3], key[3]
+            order.append(("S",) + key)
+            del ready[key]
+            now += 0.15
+            name = STAGES[piece[0]][stage]
+            if stage + 1 == len(STAGES[piece[0]]):
+                done.add(piece)
+                continue
+            us, lat, links = COST[name]
+            ready[piece + (stage + 1,)] = sent(links, us, lat)
+            continue
+        if todo and not blocked(todo[0]):
+            op = todo.pop(0)
+            order.append(op)
+            now += compute[op[0]]
+            if op[0] == "G":
+                us, lat, links = COST["send1"]
+                ready[(op[1], op[2], op[3], 0)] = sent(links, us, lat)
+            continue
+        now = max(now, min(ready.values()))
+    return order
+
+
+STAGES = (
+    ("send2", "send3", "gather3", "gather2", "gather1", "end"),
+    ("send2", "send3", "change", "gather3", "gather2", "gather1", "end"),
+)
+COST = {
+    "send1": (1.4, 1.8, "xy"),
+    "send2": (0.7, 1.8, "xy"),
+    "send3": (1.4, 3.2, "z"),
+    "change": (0.0, 1.2, ""),
+    "gather3": (1.4, 3.2, "z"),
+    "gather2": (0.7, 1.8, "xy"),
+    "gather1": (1.4, 1.8, "xy"),
+}
+
+
+def fused_kernel(
+    factor, key_ref, value_ref, rate_ref, init_ref, gain_ref, query_hbm, out_ref,
+    key_t, target, target_t, terms, weights, shard, init_down, grad, grad_bf,
+    part2, part2_bf, part3_bf, got1, got2, got3, change_mine, change_got,
+    query, y_part, query_sem, send_sem, recv_sem,
+):
+    me, place = lax.axis_index("tok"), lax.axis_index("order")
+    x, y, z = me % 2, (me // 2) % 2, me // 4
+    n_z = got3.shape[3] + 1
+    by_x = me + 1 - 2 * x
+    by_y = me + 2 - 4 * y
+    far = [((z + d) % n_z) for d in range(1, n_z)]
+    by_z = [zz * 4 + me % 4 for zz in far]
+    barrier = pltpu.get_barrier_semaphore()
+    for peer in [by_x, by_y] + by_z:
+        pl.semaphore_signal(barrier, inc=1, device_id={"tok": peer}, device_id_type=MESH)
+    pl.semaphore_signal(barrier, inc=1, device_id={"order": 1 - place}, device_id_type=MESH)
+
+    width = key_ref.shape[1]
+    cols = width // CHUNKS
+    rows = key_ref.shape[0] // PARTS
+    half = width // 2
+    fetch = pltpu.make_async_copy(query_hbm, query, query_sem)
+    fetch.start()
+
+    first, second = (x, y), (y, x)
+    peer1, peer2 = (by_x, by_y), (by_y, by_x)
+    r128 = half // 2
+    r64 = half // 4
+    r16 = r64 // n_z
+    own1 = [h * half + first[h] * r128 for h in range(2)]
+    off1 = [h * half + (1 - first[h]) * r128 for h in range(2)]
+    own2 = [own1[h] + second[h] * r64 for h in range(2)]
+    own3 = [own2[h] + z * r16 for h in range(2)]
+
+    def at(start, size):
+        return pl.ds(pl.multiple_of(start, size), size)
+
+    for c in range(CHUNKS):
+        here = slice(c * cols, (c + 1) * cols)
+        for m in range(2):
+            there = slice(m * width + c * cols, m * width + (c + 1) * cols)
+            weights[0, c, m] = init_ref[:, there].astype(jnp.bfloat16)
+        down_t = init_ref[here, 2 * width :].T
+        init_down[c] = down_t
+        weights[0, c, 2] = down_t.astype(jnp.bfloat16)
+
+    def initial(c, m, h):
+        if m == 2:
+            return init_down[c, at(own3[h], r16), :]
+        return init_ref[at(own3[h], r16), m * width + c * cols : m * width + (c + 1) * cols]
+
+    def prepare(part):
+        lines = slice(part * rows, (part + 1) * rows)
+        key_t[:, lines] = key_ref[lines, :].T
+        for b in range(part * rows // 128, (part + 1) * rows // 128):
+            here = slice(b * 128, (b + 1) * 128)
+            scale = -(jnp.broadcast_to(rate_ref[b : b + 1, :], (128, 128)).T * factor)
+            for lane in range(0, width, 128):
+                block = value_ref[here, lane : lane + 128].astype(jnp.float32)
+                target[here, lane : lane + 128] = (scale * block).astype(jnp.bfloat16)
+        target_t[:, lines] = target[lines, :].T
+
+    def elementwise(step, c, part):
+        if step == 0 and c == 0:
+            prepare(part)
+        lines = slice(part * rows, (part + 1) * rows)
+        key_rows = key_ref[lines, :]
+        gate = jnp.dot(key_rows, weights[step, c, 0], preferred_element_type=jnp.float32)
+        up = jnp.dot(key_rows, weights[step, c, 1], preferred_element_type=jnp.float32)
+        back = jnp.dot(target[lines, :], weights[step, c, 2], preferred_element_type=jnp.float32)
+        sig = jax.nn.sigmoid(gate)
+        act = gate * sig
+        terms[2, lines, :] = (act * up).astype(jnp.bfloat16)
+        terms[0, lines, :] = (back * up * sig * (1.0 + gate * (1.0 - sig))).astype(jnp.bfloat16)
+        terms[1, lines, :] = (back * act).astype(jnp.bfloat16)
+
+    def remote(src, dst, slot, device):
+        copy = pltpu.make_async_remote_copy(
+            src_ref=src, dst_ref=dst, send_sem=send_sem.at[slot], recv_sem=recv_sem.at[slot],
+            device_id=device, device_id_type=MESH,
+        )
+        copy.start()
+        return copy
+
+    flying = {}
+    greeted = []
+
+    def slot_of(c, m, k):
+        return (c * 3 + m) * (8 + 4 * n_z) + k
+
+    def gradient(step, c, m):
+        left = target_t if m == 2 else key_t
+        total = jnp.dot(left[...], terms[m], preferred_element_type=jnp.float32)
+        p = c * 3 + m
+        grad[p] = total
+        grad_bf[p] = total.astype(jnp.bfloat16)
+        if not greeted:
+            pl.semaphore_wait(barrier, 3 + len(far))
+            greeted.append(True)
+        flying[c, m] = [
+            remote(grad_bf.at[p, at(off1[h], r128), :], got1.at[step, p, h],
+                   slot_of(c, m, h), {"tok": peer1[h]})
+            for h in range(2)
+        ]
+
+    def spread3(c, m, base, source, goal):
+        return [
+            remote(source(h, d), goal(h, d), slot_of(c, m, base + h * (n_z - 1) + d), {"tok": by_z[d]})
+            for h in range(2)
+            for d in range(n_z - 1)
+        ]
+
+    def advance(step, c, m, stage):
+        p = c * 3 + m
+        name = STAGES[step][stage]
+        for copy in flying.pop((c, m)):
+            copy.wait()
+        held = weights.at[step + 1, c, m]
+        if name == "send2":
+            for h in range(2):
+                mine, other = second[h] * r64, (1 - second[h]) * r64
+                part2_bf[p, h] = (
+                    grad[p, at(own1[h] + other, r64), :] + got1[step, p, h, at(other, r64), :].astype(jnp.float32)
+                ).astype(jnp.bfloat16)
+                part2[p, h] = grad[p, at(own2[h], r64), :] + got1[step, p, h, at(mine, r64), :].astype(jnp.float32)
+            flying[c, m] = [
+                remote(part2_bf.at[p, h], got2.at[step, p, h], slot_of(c, m, 2 + h), {"tok": peer2[h]})
+                for h in range(2)
+            ]
+        elif name == "send3":
+            for h in range(2):
+                total = part2[p, h] + got2[step, p, h].astype(jnp.float32)
+                part2[p, h] = total
+                part3_bf[p, h] = total.astype(jnp.bfloat16)
+            flying[c, m] = spread3(
+                c, m, 4,
+                lambda h, d: part3_bf.at[p, h, at(far[d] * r16, r16), :],
+                lambda h, d: got3.at[step, p, h, d],
+            )
+        elif name == "change" or (name == "gather3" and step == 0):
+            for h in range(2):
+                total = part2[p, h, at(z * r16, r16), :]
+                for d in range(n_z - 1):
+                    total = total + got3[step, p, h, d].astype(jnp.float32)
+                if step == 0:
+                    fresh = initial(c, m, h) - total
+                    shard[p, h] = fresh
+                    weights[1, c, m, at(own3[h], r16), :] = fresh.astype(jnp.bfloat16)
+                else:
+                    change_mine[p, h] = (shard[p, h] - total) - initial(c, m, h)
+            if step == 1:
+                flying[c, m] = [
+                    remote(change_mine.at[p], change_got.at[p], slot_of(c, m, 4 + 4 * n_z), {"order": 1 - place})
+                ]
+        if name == "gather3":
+            if step == 1:
+                for h in range(2):
+                    earlier = jnp.where(place > 0, change_got[p, h], 0.0)
+                    closing = initial(c, m, h) + earlier + change_mine[p, h]
+                    weights[2, c, m, at(own3[h], r16), :] = closing.astype(jnp.bfloat16)
+            flying[c, m] = spread3(
+                c, m, 4 + 2 * (n_z - 1),
+                lambda h, d: held.at[at(own3[h], r16), :],
+                lambda h, d: held.at[at(own3[h], r16), :],
+            )
+        elif name in ("gather2", "gather1"):
+            wide = name == "gather1"
+            start, size = (own1, r128) if wide else (own2, r64)
+            peer = peer1 if wide else peer2
+            base = 4 + 4 * (n_z - 1) + (2 if wide else 0)
+            flying[c, m] = [
+                remote(held.at[at(start[h], size), :], held.at[at(start[h], size), :],
+                       slot_of(c, m, base + h), {"tok": peer[h]})
+                for h in range(2)
+            ]
+
+    def apply(step, c, part):
+        if c == 0 and part == 0:
+            fetch.wait()
+        lines = slice(part * rows, (part + 1) * rows)
+        rows_in = query[lines, :]
+        gate = jnp.dot(rows_in, weights[step, c, 0], preferred_element_type=jnp.float32)
+        up = jnp.dot(rows_in, weights[step, c, 1], preferred_element_type=jnp.float32)
+        hidden = (jax.nn.silu(gate) * up).astype(jnp.bfloat16)
+        result = lax.dot_general(
+            hidden, weights[step, c, 2], (((1,), (1,)), ((), ())), preferred_element_type=jnp.float32
+        )
+        if c > 0:
+            result = y_part[lines, :] + result
+        if c < CHUNKS - 1:
+            y_part[lines, :] = result
+            return
+        norm_inv = lax.rsqrt(jnp.mean(result * result, axis=1, keepdims=True) + 1e-06)
+        out_ref[lines, :] = (result * norm_inv * gain_ref[...]).astype(jnp.bfloat16)
+
+    for op in plan():
+        {"E": elementwise, "G": gradient, "S": advance, "Q": apply}[op[0]](*op[1:])
+
+
+def fused(queries, key_tokens, value_tokens, learn_rates, fast_init, out_gain):
+    tokens, width = key_tokens.shape
+    n_tok = lax.axis_size("tok")
+    n_z = n_tok // 4
+    cols = width // CHUNKS
+    pieces = 3 * CHUNKS
+    q = width // 8
+    bf, f32 = jnp.bfloat16, jnp.float32
+    factor = (tokens * n_tok) ** (-0.5)
+    sems = pieces * (8 + 4 * n_z)
+    vmem = pl.BlockSpec(memory_space=pltpu.VMEM)
+    return pl.pallas_call(
+        functools.partial(fused_kernel, factor),
+        out_shape=jax.ShapeDtypeStruct((tokens, width), bf),
+        in_specs=[vmem] * 5 + [pl.BlockSpec(memory_space=pl.ANY)],
+        out_specs=vmem,
+        scratch_shapes=[
+            pltpu.VMEM((width, tokens), bf),
+            pltpu.VMEM((tokens, width), bf),
+            pltpu.VMEM((width, tokens), bf),
+            pltpu.VMEM((3, tokens, cols), bf),
+            pltpu.VMEM((3, CHUNKS, 3, width, cols), bf),
+            pltpu.VMEM((pieces, 2, q // n_z, cols), f32),
+            pltpu.VMEM((CHUNKS, width, cols), f32),
+            pltpu.VMEM((pieces, width, cols), f32),
+            pltpu.VMEM((pieces, width, cols), bf),
+            pltpu.VMEM((pieces, 2, q, cols), f32),
+            pltpu.VMEM((pieces, 2, q, cols), bf),
+            pltpu.VMEM((pieces, 2, q, cols), bf),
+            pltpu.VMEM((2, pieces, 2, 2 * q, cols), bf),
+            pltpu.VMEM((2, pieces, 2, q, cols), bf),
+            pltpu.VMEM((2, pieces, 2, n_z - 1, q // n_z, cols), bf),
+            pltpu.VMEM((pieces, 2, q // n_z, cols), f32),
+            pltpu.VMEM((pieces, 2, q // n_z, cols), f32),
+            pltpu.VMEM((tokens, width), bf),
+            pltpu.VMEM((tokens, width), f32),
+            pltpu.SemaphoreType.DMA,
+            pltpu.SemaphoreType.DMA((sems,)),
+            pltpu.SemaphoreType.DMA((sems,)),
+        ],
+        compiler_params=pltpu.CompilerParams(
+            collective_id=0, has_side_effects=True, vmem_limit_bytes=67043328
+        ),
+    )(
+        key_tokens, value_tokens, learn_rates.reshape(-1, 128), fast_init,
+        out_gain.reshape(1, -1), queries,
+    )
+
+
 def solution(mesh):
     return jax.shard_map(
-        shards,
+        fused if tiles(mesh) else shards,
         mesh=mesh,
         in_specs=(
             P(("order", "tok"), None),

time: 383 us -> 93.4 us (0.24)
  waiting for transfers between devices: 304 us -> 0 us
  Pallas kernels: 0 us -> 90.2 us
  other arithmetic: 25.1 us -> 0 us
  matrix products: 23.8 us -> 0 us
  between operations: 13.3 us -> 0.01 us
  local copies, waits for them, and re-layouts: 14.8 us -> 3.05 us
    psum x2 -> x0, waiting for transfers between devices: 292 us -> none  [summed_whole(): return lax.psum(local_term(key_rows, hidden, inner_grads, target), 'tok')]
    pallas_call x0 -> x1, Pallas kernels: none -> 90.2 us  [fused(): pl.pallas_call(functools.partial(fused_kernel, factor), out_shape=jax.Sha...]
    dot_general x10 -> x0, matrix products: 23.8 us -> none  [the longest x3 7.18 us: gate_up(): jnp.dot(rows_in, weights_bf[:, :2 * width], preferred_element_type=jnp.fl...]
    convert_element_type x5 -> x0, other arithmetic: 20.3 us -> none  [the longest x1 6.35 us: shards(): closing_bf = (fast_init + earlier + change).astype(jnp.bfloat16)]
    all_gather x1 -> x0, waiting for transfers between devices: 11.4 us -> none  [prefix(): gathered = lax.all_gather(x.astype(jnp.bfloat16), axis)]
    while x2 -> x0, local copies, waits for them, and re-layouts: 7 us -> none  [prefix(): return lax.fori_loop(0, place, one, state)]
    concatenate x2 -> x0, other arithmetic: 3.93 us -> none  [local_term(): return jnp.concatenate([upper, lower], axis=1)]
    convert_element_type x1 -> x0, local copies, waits for them, and re-layouts: 3.92 us -> none  [apply_weights(): return (result * norm_inv * out_gain[None, :]).astype(jnp.bfloat16)]
  transfers between devices with their start and end apart: 3 -> 0, of which waited for: 3 -> 0; matrix products, arithmetic and copies ran while one was open for 1% -> 0% of each run, Pallas kernels for 0% -> 0%
where the time goes in v1:
time: 93.4 us; the launch traced here: 93.3 us
  Pallas kernels  90.2 us (97%)
  local copies, waits for them, and re-layouts  3.05 us (3%)
    pallas_call x1, Pallas kernels, fused(): pl.pallas_call(functools.partial(fused_kernel, factor), out_shape=jax.Sha...  90.2 us
    unnamed x1, local copies, waits for them, and re-layouts  3.05 us

profile of v1, /device:TPU:0, one launch (start us, length us, event | category | flops | bytes accessed | tf_op | source)
XLA Modules:
  0.0 93.3 jit_solution(12433114143345709375)
XLA Ops:
  0.0 90.2 %shard_map.64 = bf16[2048,512]{1,0:T(8,128)(2,1)} custom-call(bf16[2048,512]{1,0:T(8,128)(2,1)} %key_ref.1, bf16[2048,512]{1,0:T(8,128)(2,1)} %value_ref.1, f32[16,128]{1,0:T(8,128)} %bitcast.2, f32[512,1536]{1,0:T(8,128)} %init_ref.1, f32[1,512]{1,0:T(1,128)} %bitcast.3, bf16[2048,512]{1,0:T(8,128)(2,1)} %query_hbm.1), custom_call_target="tpu_custom_call" | custom-call | tf_op jit(solution)/shard_map/pallas_call | solution.py:379
  90.2 3.0 %copy.8 = bf16[2048,512]{1,0:T(8,128)(2,1)} copy(bf16[2048,512]{1,0:T(8,128)(2,1)} %shard_map.64) | data formatting | bytes 4194304

commit v2 on v1

--- a/solution.py
+++ b/solution.py
@@ -7,7 +7,7 @@
 from jax.experimental.pallas import tpu as pltpu
 from jax.sharding import PartitionSpec as P
 
-CHUNKS = 2
+CHUNKS = 4
 PARTS = 4
 MESH = pl.DeviceIdType.MESH
 
@@ -95,7 +95,7 @@
 
 
 def plan():
-    compute = {"T": 1.0, "E": 0.9, "G": 0.8, "Q": 0.9}
+    compute = {"E": 0.6, "G": 1.0, "Q": 0.6}
     wire = {"x": 0.0, "y": 0.0, "z": 0.0}
     order, now = [], 0.0
     ready, done = {}, set()
@@ -104,8 +104,7 @@
         for c in range(CHUNKS):
             for part in range(PARTS):
                 todo.append(("E", step, c, part))
-            for m in (2, 0, 1):
-                todo.append(("G", step, c, m))
+            todo.append(("G", step, c))
     for c in range(CHUNKS):
         for part in range(PARTS):
             todo.append(("Q", 2, c, part))
@@ -120,14 +119,13 @@
     def blocked(op):
         if op[0] == "G" or op[1] == 0:
             return False
-        return not all((op[1] - 1, op[2], m) in done for m in range(3))
-
-    last = {0: 6, 1: 7}
+        return (op[1] - 1, op[2]) not in done
+
     while todo or ready:
         due = sorted((when, key) for key, when in ready.items() if when <= now + 0.05)
         if due:
             key = due[0][1]
-            piece, stage = key[:3], key[3]
+            piece, stage = key[:2], key[2]
             order.append(("S",) + key)
             del ready[key]
             now += 0.15
@@ -144,7 +142,7 @@
             now += compute[op[0]]
             if op[0] == "G":
                 us, lat, links = COST["send1"]
-                ready[(op[1], op[2], op[3], 0)] = sent(links, us, lat)
+                ready[(op[1], op[2], 0)] = sent(links, us, lat)
             continue
         now = max(now, min(ready.values()))
     return order
@@ -155,21 +153,21 @@
     ("send2", "send3", "change", "gather3", "gather2", "gather1", "end"),
 )
 COST = {
-    "send1": (1.4, 1.8, "xy"),
-    "send2": (0.7, 1.8, "xy"),
-    "send3": (1.4, 3.2, "z"),
-    "change": (0.0, 1.2, ""),
-    "gather3": (1.4, 3.2, "z"),
-    "gather2": (0.7, 1.8, "xy"),
-    "gather1": (1.4, 1.8, "xy"),
+    "send1": (2.1, 2.2, "xy"),
+    "send2": (1.0, 2.2, "xy"),
+    "send3": (2.1, 3.6, "z"),
+    "change": (0.0, 1.4, ""),
+    "gather3": (2.1, 3.6, "z"),
+    "gather2": (1.0, 2.2, "xy"),
+    "gather1": (2.1, 2.2, "xy"),
 }
 
 
 def fused_kernel(
-    factor, key_ref, value_ref, rate_ref, init_ref, gain_ref, query_hbm, out_ref,
+    factor, key_hbm, value_hbm, rate_ref, init_hbm, gain_ref, query_hbm, out_ref,
     key_t, target, target_t, terms, weights, shard, init_down, grad, grad_bf,
     part2, part2_bf, part3_bf, got1, got2, got3, change_mine, change_got,
-    query, y_part, query_sem, send_sem, recv_sem,
+    key_ref, value_ref, init_ref, query, y_part, load_sem, send_sem, recv_sem,
 ):
     me, place = lax.axis_index("tok"), lax.axis_index("order")
     x, y, z = me % 2, (me // 2) % 2, me // 4
@@ -187,8 +185,18 @@
     cols = width // CHUNKS
     rows = key_ref.shape[0] // PARTS
     half = width // 2
-    fetch = pltpu.make_async_copy(query_hbm, query, query_sem)
-    fetch.start()
+    loads = []
+
+    def load(src, dst):
+        loads.append(pltpu.make_async_copy(src, dst, load_sem.at[len(loads)]))
+        loads[-1].start()
+
+    load(init_hbm, init_ref)
+    for part in range(PARTS):
+        lines = slice(part * rows, (part + 1) * rows)
+        load(key_hbm.at[lines], key_ref.at[lines])
+        load(value_hbm.at[lines], value_ref.at[lines])
+    loads[0].wait()
 
     first, second = (x, y), (y, x)
     peer1, peer2 = (by_x, by_y), (by_y, by_x)
@@ -203,19 +211,25 @@
     def at(start, size):
         return pl.ds(pl.multiple_of(start, size), size)
 
-    for c in range(CHUNKS):
+    def cast(c):
         here = slice(c * cols, (c + 1) * cols)
         for m in range(2):
             there = slice(m * width + c * cols, m * width + (c + 1) * cols)
-            weights[0, c, m] = init_ref[:, there].astype(jnp.bfloat16)
+            weights[0, c, :, m * cols : (m + 1) * cols] = init_ref[:, there].astype(jnp.bfloat16)
         down_t = init_ref[here, 2 * width :].T
         init_down[c] = down_t
-        weights[0, c, 2] = down_t.astype(jnp.bfloat16)
-
-    def initial(c, m, h):
-        if m == 2:
-            return init_down[c, at(own3[h], r16), :]
-        return init_ref[at(own3[h], r16), m * width + c * cols : m * width + (c + 1) * cols]
+        weights[0, c, :, 2 * cols :] = down_t.astype(jnp.bfloat16)
+
+    def initial(c, h):
+        mine = at(own3[h], r16)
+        return jnp.concatenate(
+            [
+                init_ref[mine, c * cols : (c + 1) * cols],
+                init_ref[mine, width + c * cols : width + (c + 1) * cols],
+                init_down[c, mine, :],
+            ],
+            axis=1,
+        )
 
     def prepare(part):
         lines = slice(part * rows, (part + 1) * rows)
@@ -229,18 +243,27 @@
         target_t[:, lines] = target[lines, :].T
 
     def elementwise(step, c, part):
+        if step == 0 and part == 0:
+            cast(c)
         if step == 0 and c == 0:
+            loads[1 + 2 * part].wait()
+            loads[2 + 2 * part].wait()
             prepare(part)
+            if part == PARTS - 1:
+                load(query_hbm, query)
         lines = slice(part * rows, (part + 1) * rows)
         key_rows = key_ref[lines, :]
-        gate = jnp.dot(key_rows, weights[step, c, 0], preferred_element_type=jnp.float32)
-        up = jnp.dot(key_rows, weights[step, c, 1], preferred_element_type=jnp.float32)
-        back = jnp.dot(target[lines, :], weights[step, c, 2], preferred_element_type=jnp.float32)
+        both = jnp.dot(key_rows, weights[step, c, :, : 2 * cols], preferred_element_type=jnp.float32)
+        gate, up = both[:, :cols], both[:, cols:]
+        back = jnp.dot(
+            target[lines, :], weights[step, c, :, 2 * cols :], preferred_element_type=jnp.float32
+        )
         sig = jax.nn.sigmoid(gate)
         act = gate * sig
-        terms[2, lines, :] = (act * up).astype(jnp.bfloat16)
-        terms[0, lines, :] = (back * up * sig * (1.0 + gate * (1.0 - sig))).astype(jnp.bfloat16)
-        terms[1, lines, :] = (back * act).astype(jnp.bfloat16)
+        slope = back * up * sig * (1.0 + gate * (1.0 - sig))
+        terms[lines, :cols] = slope.astype(jnp.bfloat16)
+        terms[lines, cols : 2 * cols] = (back * act).astype(jnp.bfloat16)
+        terms[lines, 2 * cols :] = (act * up).astype(jnp.bfloat16)
 
     def remote(src, dst, slot, device):
         copy = pltpu.make_async_remote_copy(
@@ -253,37 +276,39 @@
     flying = {}
     greeted = []
 
-    def slot_of(c, m, k):
-        return (c * 3 + m) * (8 + 4 * n_z) + k
-
-    def gradient(step, c, m):
-        left = target_t if m == 2 else key_t
-        total = jnp.dot(left[...], terms[m], preferred_element_type=jnp.float32)
-        p = c * 3 + m
-        grad[p] = total
-        grad_bf[p] = total.astype(jnp.bfloat16)
+    def slot_of(c, k):
+        return c * (8 + 4 * n_z) + k
+
+    def gradient(step, c):
+        upper = jnp.dot(key_t[...], terms[:, : 2 * cols], preferred_element_type=jnp.float32)
+        lower = jnp.dot(target_t[...], terms[:, 2 * cols :], preferred_element_type=jnp.float32)
+        p = c
+        grad[p, :, : 2 * cols] = upper
+        grad[p, :, 2 * cols :] = lower
+        grad_bf[p, :, : 2 * cols] = upper.astype(jnp.bfloat16)
+        grad_bf[p, :, 2 * cols :] = lower.astype(jnp.bfloat16)
         if not greeted:
             pl.semaphore_wait(barrier, 3 + len(far))
             greeted.append(True)
-        flying[c, m] = [
+        flying[c] = [
             remote(grad_bf.at[p, at(off1[h], r128), :], got1.at[step, p, h],
-                   slot_of(c, m, h), {"tok": peer1[h]})
+                   slot_of(c, h), {"tok": peer1[h]})
             for h in range(2)
         ]
 
-    def spread3(c, m, base, source, goal):
+    def spread3(c, base, source, goal):
         return [
-            remote(source(h, d), goal(h, d), slot_of(c, m, base + h * (n_z - 1) + d), {"tok": by_z[d]})
+            remote(source(h, d), goal(h, d), slot_of(c, base + h * (n_z - 1) + d), {"tok": by_z[d]})
             for h in range(2)
             for d in range(n_z - 1)
         ]
 
-    def advance(step, c, m, stage):
-        p = c * 3 + m
+    def advance(step, c, stage):
+        p = c
         name = STAGES[step][stage]
-        for copy in flying.pop((c, m)):
+        for copy in flying.pop(c):
             copy.wait()
-        held = weights.at[step + 1, c, m]
+        held = weights.at[step + 1, c]
         if name == "send2":
             for h in range(2):
                 mine, other = second[h] * r64, (1 - second[h]) * r64
@@ -291,8 +316,8 @@
                     grad[p, at(own1[h] + other, r64), :] + got1[step, p, h, at(other, r64), :].astype(jnp.float32)
                 ).astype(jnp.bfloat16)
                 part2[p, h] = grad[p, at(own2[h], r64), :] + got1[step, p, h, at(mine, r64), :].astype(jnp.float32)
-            flying[c, m] = [
-                remote(part2_bf.at[p, h], got2.at[step, p, h], slot_of(c, m, 2 + h), {"tok": peer2[h]})
+            flying[c] = [
+                remote(part2_bf.at[p, h], got2.at[step, p, h], slot_of(c, 2 + h), {"tok": peer2[h]})
                 for h in range(2)
             ]
         elif name == "send3":
@@ -300,8 +325,8 @@
                 total = part2[p, h] + got2[step, p, h].astype(jnp.float32)
                 part2[p, h] = total
                 part3_bf[p, h] = total.astype(jnp.bfloat16)
-            flying[c, m] = spread3(
-                c, m, 4,
+            flying[c] = spread3(
+                c, 4,
                 lambda h, d: part3_bf.at[p, h, at(far[d] * r16, r16), :],
                 lambda h, d: got3.at[step, p, h, d],
             )
@@ -311,23 +336,23 @@
                 for d in range(n_z - 1):
                     total = total + got3[step, p, h, d].astype(jnp.float32)
                 if step == 0:
-                    fresh = initial(c, m, h) - total
+                    fresh = initial(c, h) - total
                     shard[p, h] = fresh
-                    weights[1, c, m, at(own3[h], r16), :] = fresh.astype(jnp.bfloat16)
+                    weights[1, c, at(own3[h], r16), :] = fresh.astype(jnp.bfloat16)
                 else:
-                    change_mine[p, h] = (shard[p, h] - total) - initial(c, m, h)
+                    change_mine[p, h] = (shard[p, h] - total) - initial(c, h)
             if step == 1:
-                flying[c, m] = [
-                    remote(change_mine.at[p], change_got.at[p], slot_of(c, m, 4 + 4 * n_z), {"order": 1 - place})
+                flying[c] = [
+                    remote(change_mine.at[p], change_got.at[p], slot_of(c, 4 + 4 * n_z), {"order": 1 - place})
                 ]
         if name == "gather3":
             if step == 1:
                 for h in range(2):
                     earlier = jnp.where(place > 0, change_got[p, h], 0.0)
-                    closing = initial(c, m, h) + earlier + change_mine[p, h]
-                    weights[2, c, m, at(own3[h], r16), :] = closing.astype(jnp.bfloat16)
-            flying[c, m] = spread3(
-                c, m, 4 + 2 * (n_z - 1),
+                    closing = initial(c, h) + earlier + change_mine[p, h]
+                    weights[2, c, at(own3[h], r16), :] = closing.astype(jnp.bfloat16)
+            flying[c] = spread3(
+                c, 4 + 2 * (n_z - 1),
                 lambda h, d: held.at[at(own3[h], r16), :],
                 lambda h, d: held.at[at(own3[h], r16), :],
             )
@@ -336,22 +361,22 @@
             start, size = (own1, r128) if wide else (own2, r64)
             peer = peer1 if wide else peer2
             base = 4 + 4 * (n_z - 1) + (2 if wide else 0)
-            flying[c, m] = [
+            flying[c] = [
                 remote(held.at[at(start[h], size), :], held.at[at(start[h], size), :],
-                       slot_of(c, m, base + h), {"tok": peer[h]})
+                       slot_of(c, base + h), {"tok": peer[h]})
                 for h in range(2)
             ]
 
     def apply(step, c, part):
         if c == 0 and part == 0:
-            fetch.wait()
+            loads[-1].wait()
         lines = slice(part * rows, (part + 1) * rows)
         rows_in = query[lines, :]
-        gate = jnp.dot(rows_in, weights[step, c, 0], preferred_element_type=jnp.float32)
-        up = jnp.dot(rows_in, weights[step, c, 1], preferred_element_type=jnp.float32)
+        both = jnp.dot(rows_in, weights[step, c, :, : 2 * cols], preferred_element_type=jnp.float32)
+        gate, up = both[:, :cols], both[:, cols:]
         hidden = (jax.nn.silu(gate) * up).astype(jnp.bfloat16)
         result = lax.dot_general(
-            hidden, weights[step, c, 2], (((1,), (1,)), ((), ())), preferred_element_type=jnp.float32
+            hidden, weights[step, c, :, 2 * cols :], (((1,), (1,)), ((), ())), preferred_element_type=jnp.float32
         )
         if c > 0:
             result = y_part[lines, :] + result
@@ -370,38 +395,42 @@
     n_tok = lax.axis_size("tok")
     n_z = n_tok // 4
     cols = width // CHUNKS
-    pieces = 3 * CHUNKS
+    deep = 3 * cols
     q = width // 8
     bf, f32 = jnp.bfloat16, jnp.float32
     factor = (tokens * n_tok) ** (-0.5)
-    sems = pieces * (8 + 4 * n_z)
+    sems = CHUNKS * (8 + 4 * n_z)
+    hbm = pl.BlockSpec(memory_space=pl.ANY)
     vmem = pl.BlockSpec(memory_space=pltpu.VMEM)
     return pl.pallas_call(
         functools.partial(fused_kernel, factor),
         out_shape=jax.ShapeDtypeStruct((tokens, width), bf),
-        in_specs=[vmem] * 5 + [pl.BlockSpec(memory_space=pl.ANY)],
+        in_specs=[hbm, hbm, vmem, hbm, vmem, hbm],
         out_specs=vmem,
         scratch_shapes=[
             pltpu.VMEM((width, tokens), bf),
             pltpu.VMEM((tokens, width), bf),
             pltpu.VMEM((width, tokens), bf),
-            pltpu.VMEM((3, tokens, cols), bf),
-            pltpu.VMEM((3, CHUNKS, 3, width, cols), bf),
-            pltpu.VMEM((pieces, 2, q // n_z, cols), f32),
+            pltpu.VMEM((tokens, deep), bf),
+            pltpu.VMEM((3, CHUNKS, width, deep), bf),
+            pltpu.VMEM((CHUNKS, 2, q // n_z, deep), f32),
             pltpu.VMEM((CHUNKS, width, cols), f32),
-            pltpu.VMEM((pieces, width, cols), f32),
-            pltpu.VMEM((pieces, width, cols), bf),
-            pltpu.VMEM((pieces, 2, q, cols), f32),
-            pltpu.VMEM((pieces, 2, q, cols), bf),
-            pltpu.VMEM((pieces, 2, q, cols), bf),
-            pltpu.VMEM((2, pieces, 2, 2 * q, cols), bf),
-            pltpu.VMEM((2, pieces, 2, q, cols), bf),
-            pltpu.VMEM((2, pieces, 2, n_z - 1, q // n_z, cols), bf),
-            pltpu.VMEM((pieces, 2, q // n_z, cols), f32),
-            pltpu.VMEM((pieces, 2, q // n_z, cols), f32),
+            pltpu.VMEM((CHUNKS, width, deep), f32),
+            pltpu.VMEM((CHUNKS, width, deep), bf),
+            pltpu.VMEM((CHUNKS, 2, q, deep), f32),
+            pltpu.VMEM((CHUNKS, 2, q, deep), bf),
+            pltpu.VMEM((CHUNKS, 2, q, deep), bf),
+            pltpu.VMEM((2, CHUNKS, 2, 2 * q, deep), bf),
+            pltpu.VMEM((2, CHUNKS, 2, q, deep), bf),
+            pltpu.VMEM((2, CHUNKS, 2, n_z - 1, q // n_z, deep), bf),
+            pltpu.VMEM((CHUNKS, 2, q // n_z, deep), f32),
+            pltpu.VMEM((CHUNKS, 2, q // n_z, deep), f32),
+            pltpu.VMEM((tokens, width), bf),
+            pltpu.VMEM((tokens, width), bf),
+            pltpu.VMEM((width, 3 * width), f32),
             pltpu.VMEM((tokens, width), bf),
             pltpu.VMEM((tokens, width), f32),
-            pltpu.SemaphoreType.DMA,
+            pltpu.SemaphoreType.DMA((2 + 2 * PARTS,)),
             pltpu.SemaphoreType.DMA((sems,)),
             pltpu.SemaphoreType.DMA((sems,)),
         ],

time: 93.4 us -> 90.6 us (0.970)
  Pallas kernels: 90.2 us -> 87.4 us
    pallas_call x1, Pallas kernels: 90.2 us -> 87.4 us  [fused(): pl.pallas_call(functools.partial(fused_kernel, factor), out_shape=jax.Sha...]
where the time goes in v2:
time: 90.6 us; the launch traced here: 90.4 us
  Pallas kernels  87.4 us (96%)
  local copies, waits for them, and re-layouts  3.05 us (3%)
    pallas_call x1, Pallas kernels, fused(): pl.pallas_call(functools.partial(fused_kernel, factor), out_shape=jax.Sha...  87.4 us
    unnamed x1, local copies, waits for them, and re-layouts  3.05 us

profile of v2, /device:TPU:0, one launch (start us, length us, event | category | flops | bytes accessed | tf_op | source)
XLA Modules:
  0.0 90.4 jit_solution(15867606815189948774)
XLA Ops:
  0.0 87.4 %shard_map.64 = bf16[2048,512]{1,0:T(8,128)(2,1)} custom-call(bf16[2048,512]{1,0:T(8,128)(2,1)} %key_hbm.1, bf16[2048,512]{1,0:T(8,128)(2,1)} %value_hbm.1, f32[16,128]{1,0:T(8,128)} %bitcast.2, f32[512,1536]{1,0:T(8,128)} %init_hbm.1, f32[1,512]{1,0:T(1,128)} %bitcast.3, bf16[2048,512]{1,0:T(8,128)(2,1)} %query_hbm.1), custom_call_target="tpu_custom_call" | custom-call | tf_op jit(solution)/shard_map/pallas_call | solution.py:405
  87.4 3.0 %copy.8 = bf16[2048,512]{1,0:T(8,128)(2,1)} copy(bf16[2048,512]{1,0:T(8,128)(2,1)} %shard_map.64) | data formatting | bytes 4194304
